TPU v7x, 256 devices: a whole 4x4x8 slice. The times are simulated.
256 devices in a mesh: shot: 64 (over y, z_hi, x), rcv: 4 (over z_lo, core).
Axes of the slice: x: 4, y: 4, z: 8 (z_hi: 4, z_lo: 2; z = z_hi * 2 + z_lo), core: 2. Of those that a mesh axis runs over, the one named last changes fastest.
Arguments:
- data: bfloat16 [384, 1024, 256], P('shot', 'rcv'), may hold values from -6 to 6
- surface_traces: bfloat16 [1024, 1024, 256], P('shot', 'rcv'), may hold values from -6 to 6
- primaries: bfloat16 [384, 64, 64], P('shot', 'rcv'), may hold values from -0.09375 to 0.09375
- panel_owner: int32 [4], replicated, may hold values from 0 to 63, as said below
Outputs:
- residual: bfloat16 [384, 1024, 256], P('shot', 'rcv')
Inputs may be any that keep to these rules, and one draw needn't show every extreme that they name: panel_owner holds 4 distinct indices of the shot axis, in an order drawn from the seed.
All inputs are finite; a program needn't handle non-finite values.
Results may differ from a plain program's by a relative error of at most 0.001.
Values may be sent and summed in bfloat16 or wider, within the bound.
A program may use at most 128 MiB of HBM per device.

v0:
```python
import jax
import jax.numpy as jnp
from jax import lax
from jax.sharding import PartitionSpec as P

TAPS = 64
KP = 16
PANELS = 4
BLOCK = 128


def broadcast(value, axis, root):
    mine = lax.axis_index(axis) == root
    return lax.psum(jnp.where(mine, value, jnp.zeros_like(value)), axis)


def shift_table(taps, block):
    lag_index = lax.broadcasted_iota(jnp.int32, (2, taps, block, block), 0)
    tap_index = lax.broadcasted_iota(jnp.int32, (2, taps, block, block), 1)
    in_index = lax.broadcasted_iota(jnp.int32, (2, taps, block, block), 2)
    out_index = lax.broadcasted_iota(jnp.int32, (2, taps, block, block), 3)
    distance = out_index - in_index + lag_index * block
    return (distance == tap_index).astype(jnp.bfloat16)


def band_matrices(panel_prim, shift_ones):
    bands = jnp.einsum(
        "skt,ltio->lskio", panel_prim, shift_ones, preferred_element_type=jnp.float32
    )
    return bands.astype(jnp.bfloat16)


def convolve(traces, bands, block):
    point_count, row_count, length = traces.shape
    blocks = traces.reshape(point_count, row_count, length // block, block)
    earlier = jnp.concatenate([jnp.zeros_like(blocks[:, :, :1]), blocks[:, :, :-1]], axis=2)
    stacked = jnp.stack([blocks, earlier])
    product = jnp.einsum("lkrbi,lskio->srbo", stacked, bands, preferred_element_type=jnp.float32)
    return product.reshape(bands.shape[1], row_count, length)


def shards(data, surface_traces, primaries, panel_owner):
    shift_ones = shift_table(TAPS, BLOCK)
    summed = jnp.zeros(data.shape, jnp.float32)
    panels_here = primaries.shape[1] // KP
    for panel_id in range(PANELS):
        first_point = panel_id % panels_here * KP
        panel_prim = broadcast(primaries, "rcv", panel_id // panels_here)
        traces = broadcast(surface_traces, "shot", panel_owner[panel_id])
        summed = summed + convolve(traces, band_matrices(panel_prim, shift_ones), BLOCK)
    return (data.astype(jnp.float32) - summed).astype(jnp.bfloat16)


def solution(mesh):
    placed = (P("shot", "rcv", None), P("shot", "rcv", None), P("shot", "rcv", None), P())
    return jax.shard_map(
        shards, mesh=mesh, in_specs=placed, out_specs=P("shot", "rcv", None), check_vma=False
    )
```

profile of v0, /device:TPU:2, one launch (start us, length us, event | category | flops | bytes accessed | tf_op | source)
XLA Modules:
  0.0 849.8 jit_solution(237345734642141032)
XLA Ops:
  6.5 1.5 fusion.39
  10.6 2.9 copy.6
  13.5 3.5 broadcast_select_fusion.3
  17.0 0.7 copy-done.9
  17.7 12.9 %all-reduce.5 = (bf16[6,16,64]{2,1,0:T(8,128)(2,1)S(1)}, bf16[6,16,64]{2,1,0:T(8,128)(2,1)S(1)}, bf16[6,16,64]{2,1,0:T(8,128)(2,1)S(1)}, bf16[6,16,64]{2,1,0:T(8,128)(2,1)S(1)}) all-reduce(bf16[6,16,64]{2,1,0:T(8,128)(2,1)S(1)} %get-tuple-element.19, ...), channel_id=1, replica_groups=mesh['shot'=64,'rcv'=4] {'rcv'}, use_global_device_ids=true, to_apply=%region_6.7 | all-reduce | flops 24576 | bytes 98304 | tf_op jit(solution)/shard_map/psum | solution.py:14
  30.6 1.5 fusion
  32.1 6.4 fusion.25
  38.5 9.2 %copy.25 = bf16[2,128,128,6,16]{1,2,0,4,3:T(8,128)(2,1)} copy(bf16[2,128,128,6,16]{2,4,3,1,0:T(8,128)(2,1)} %fusion.25) | data formatting | bytes 12582912 | tf_op jit(solution)/shard_map/skt,ltio->lskio/dot_general | solution.py:27
  47.6 6.4 fusion.23
  54.0 9.2 %copy.29 = bf16[2,128,128,6,16]{1,2,0,4,3:T(8,128)(2,1)} copy(bf16[2,128,128,6,16]{2,4,3,1,0:T(8,128)(2,1)} %fusion.23) | data formatting | bytes 12582912 | tf_op jit(solution)/shard_map/skt,ltio->lskio/dot_general | solution.py:27
  63.3 6.3 fusion.21
  69.6 9.2 %copy.33 = bf16[2,128,128,6,16]{1,2,0,4,3:T(8,128)(2,1)} copy(bf16[2,128,128,6,16]{2,4,3,1,0:T(8,128)(2,1)} %fusion.21) | data formatting | bytes 12582912 | tf_op jit(solution)/shard_map/skt,ltio->lskio/dot_general | solution.py:27
  78.8 6.4 fusion.27
  85.2 9.2 %copy.21 = bf16[2,128,128,6,16]{1,2,0,4,3:T(8,128)(2,1)} copy(bf16[2,128,128,6,16]{2,4,3,1,0:T(8,128)(2,1)} %fusion.27) | data formatting | bytes 12582912 | tf_op jit(solution)/shard_map/skt,ltio->lskio/dot_general | solution.py:27
  94.4 700.7 %all-reduce.8.cloned.1.call-done = (bf16[16,256,256]{1,2,0:T(8,128)(2,1)}, bf16[16,256,256]{1,2,0:T(8,128)(2,1)}, bf16[16,256,256]{1,2,0:T(8,128)(2,1)}, bf16[16,256,256]{1,2,0:T(8,128)(2,1)}) async-done(((bf16[16,256,256]{1,2,0:T(8,128)(2,1)}, bf16[16,256,256]{1,2,0:T(8,128)(2,1)}, bf16[16,256,256]{1,2,0:T(8,128)(2,1)}, bf16[16,256,256]{1,2,0:T(8,128)(2,1)}), (bf16[16,256,256]{1,2,0:T(8,128)(2,1)}, ...) | async-done | bytes 8388624 | tf_op jit(solution)/shard_map/psum | solution.py:14
  795.1 1.3 slice.33
  796.4 0.7 copy.37
  797.1 1.7 pad_bitcast_fusion.2
  798.8 4.1 copy.11
  803.0 0.7 copy.38
  803.6 1.7 pad_bitcast_fusion.1
  805.3 4.1 copy.14
  809.5 0.7 copy.39
  810.1 1.7 pad_bitcast_fusion
  811.9 4.1 copy.17
  816.7 1.6 pad_bitcast_fusion.3
  818.4 4.1 copy.8
  822.5 7.2 fusion.5
  829.8 3.4 fusion.3
  833.3 3.4 fusion.1
  836.8 3.4 bitcast_add_fusion
  840.7 2.2 subtract_convert_fusion
  (43 shorter events, 1.5 us)
Async XLA Ops:
  6.5 788.6 %all-reduce.8.cloned.1.call-start = ((), (), s32[]{:S(2)}) async-start(), calls=%async_computation | async-start | bytes 16777216 | tf_op jit(solution)/shard_map/psum | solution.py:14
  16.9 0.7 copy-start.9
  798.8 4.1 copy-start.2
  805.3 4.1 copy-start.1
  811.9 4.1 copy-start
  818.4 11.4 %slice-start = ((s8[6291456]{0:T(1024)(128)(4,1)}), s8[2097152]{0:T(1024)(128)(4,1)S(1)}, s32[]{:S(2)}) async-start(s8[6291456]{0:T(1024)(128)(4,1)} %bitcast.109), calls=%async_computation.1 | async-start | bytes 4194304
  822.5 7.3 slice-start.1
  822.5 7.3 copy-start.3
  822.5 7.3 copy-start.6
  822.5 10.8 %slice-start.2 = ((s8[6291456]{0:T(1024)(128)(4,1)}), s8[4194304]{0:T(1024)(128)(4,1)S(1)}, s32[]{:S(2)}) async-start(s8[6291456]{0:T(1024)(128)(4,1)} %bitcast.111), calls=%async_computation.3 | async-start | bytes 8388608
  829.8 3.5 slice-start.3
  829.8 3.5 copy-start.4
  829.8 3.5 copy-start.7
  829.8 7.0 slice-start.4
  833.3 3.5 slice-start.5
  833.3 3.5 copy-start.5
  833.3 3.5 copy-start.8
Sparse Core Ops, SparseCore 0:
  17.1 777.9 all-reduce.7
where the time goes:
time: 855 us; the launch traced here: 850 us
  waiting for transfers between devices  701 us (82%)
  local copies, waits for them, and re-layouts  69.6 us (8%)
  matrix products  43.1 us (5%)
  between operations  16.3 us (2%)
  blocking collectives  12.9 us (2%)
    psum x1, waiting for transfers between devices, broadcast(): return lax.psum(jnp.where(mine, value, jnp.zeros_like(value)), axis)  701 us
    dot_general x4, local copies, waits for them, and re-layouts, band_matrices(): jnp.einsum('skt,ltio->lskio', panel_prim, shift_ones, preferred_element_t...  36.8 us
    dot_general x4, matrix products, band_matrices(): jnp.einsum('skt,ltio->lskio', panel_prim, shift_ones, preferred_element_t...  25.5 us
    another operation x8, local copies, waits for them, and re-layouts, convolve(): stacked = jnp.stack([blocks, earlier])  23 us
    dot_general x4, matrix products, convolve(): jnp.einsum('lkrbi,lskio->srbo', stacked, bands, preferred_element_type=jn...  17.5 us
  transfers between devices with their start and end apart: 1, of which 1 were waited for; matrix products, arithmetic and copies ran while one was open for 8% of the time, Pallas kernels for 0%

commit v1 on v0

v1 whole, which is shorter than its diff:
```python
import functools

import jax
import jax.numpy as jnp
from jax import lax
from jax.experimental import pallas as pl
from jax.experimental.pallas import tpu as pltpu
from jax.sharding import PartitionSpec as P

NY, NZ, NX = 4, 4, 4
NR = 4
PLANE = NY * NX
TAPS = 64
LANES = 128
CHUNKS = 4


def shot_index(y, z, x):
    return (y * NZ + z) * NX + x


def kernel(owner, traces, prim_in, data, out, ra, sb, rb, win, prim, prim32, band, acc,
           own_sem, pa_send, pa_recv, pb_send, pb_recv, zg_send, zg_recv,
           pr_own, pr_send, pr_recv, xy_send, s1, f1, s2, f2):
    rows = data.shape[1]
    shots = data.shape[0]
    size = rows // CHUNKS
    shot = lax.axis_index("shot")
    rcv = lax.axis_index("rcv")
    my_x = lax.rem(shot, NX)
    my_z = lax.rem(shot // NX, NZ)
    my_y = shot // (NX * NZ)
    my_q = my_y * NX + my_x

    def at(dy, dz, dx):
        y = lax.rem(my_y + dy, NY)
        z = lax.rem(my_z + dz, NZ)
        x = lax.rem(my_x + dx, NX)
        return shot_index(y, z, x), y * NX + x, z

    plane = [(dy, dx) for dy in range(NY) for dx in range(NX) if dy or dx]
    order = sorted(plane, key=lambda d: -(min(d[0], NY - d[0]) + min(d[1], NX - d[1])))

    barrier = pltpu.get_barrier_semaphore()
    for dy, dx in plane:
        pl.semaphore_signal(barrier, inc=1, device_id={"shot": at(dy, 0, dx)[0]})
    for dz in range(1, NZ):
        pl.semaphore_signal(barrier, inc=1, device_id={"shot": at(0, dz, 0)[0]})
    for dr in range(1, NR):
        pl.semaphore_signal(barrier, inc=1, device_id={"rcv": lax.rem(rcv + dr, NR)})
    pl.semaphore_wait(barrier, len(plane) + NZ - 1 + NR - 1)

    def part(c):
        return pl.ds(c * size, size)

    pltpu.make_async_copy(prim_in, prim.at[rcv], pr_own).start()
    for dr in range(1, NR):
        pltpu.make_async_remote_copy(
            src_ref=prim_in, dst_ref=prim.at[rcv], send_sem=pr_send.at[dr], recv_sem=pr_recv.at[dr],
            device_id={"rcv": lax.rem(rcv + dr, NR)}).start()

    for c in range(CHUNKS):
        pltpu.make_async_copy(traces.at[my_q, part(c)], ra[c].at[my_q], own_sem.at[c]).start()
        for dy, dx in order:
            device, q, _ = at(dy, 0, dx)
            pltpu.make_async_remote_copy(
                src_ref=traces.at[q, part(c)], dst_ref=ra[c].at[my_q],
                send_sem=pa_send.at[c], recv_sem=pa_recv.at[c], device_id={"shot": device}).start()

    pltpu.make_async_copy(prim_in, prim.at[rcv], pr_own).wait()
    for dr in range(1, NR):
        pltpu.make_async_copy(prim_in, prim.at[0], pr_recv.at[dr]).wait()
    prim32[...] = jnp.zeros_like(prim32)
    prim32[:, :, :, 0:TAPS] = prim[...].astype(jnp.float32)

    def make_bands(q, carry):
        for h in range(4):
            for s in range(shots):
                row = prim32[h, s, pl.ds(q, 1), :]
                tile = pltpu.roll(jnp.broadcast_to(row, (TAPS, LANES)), 0, 1, stride=1, stride_axis=0)
                start = pl.multiple_of(q * (4 * TAPS) + h * TAPS, TAPS)
                band[pl.ds(start, TAPS), s * LANES:(s + 1) * LANES] = tile.astype(jnp.bfloat16)
        return carry

    lax.fori_loop(0, PLANE, make_bands, 0)

    def gathered(buffer, count, sem, c):
        piece = buffer.at[pl.ds(0, count), part(c)]
        pltpu.make_async_copy(piece, piece, sem).wait()

    def split(index):
        return index // (NX * NZ) * NX + lax.rem(index, NX), lax.rem(index // NX, NZ)

    def stage_plane(c):
        pltpu.make_async_copy(traces.at[0, part(c)], ra[c].at[0], own_sem.at[c]).wait()
        gathered(win, PLANE - 1, pa_recv.at[c], c)
        for h in range(NZ):
            sb[h, part(c)] = ra[c][split(owner[h])[0]]
        for dz in range(1, NZ):
            device, _, z = at(0, dz, 0)
            pltpu.make_async_remote_copy(
                src_ref=sb.at[z, part(c)], dst_ref=rb[c].at[my_z],
                send_sem=pb_send.at[c], recv_sem=pb_recv.at[c], device_id={"shot": device}).start()
        rb[c][my_z] = sb[my_z, part(c)]

    def stage_column(c):
        gathered(win, NZ - 1, pb_recv.at[c], c)
        mine = my_q * NZ + my_z
        win[mine, part(c)] = rb[c][split(owner[my_z])[1]]
        for dz in range(1, NZ):
            device, _, _ = at(0, dz, 0)
            piece = win.at[mine, part(c)]
            pltpu.make_async_remote_copy(
                src_ref=piece, dst_ref=piece,
                send_sem=zg_send.at[c], recv_sem=zg_recv.at[c], device_id={"shot": device}).start()

    def step(kind, first, second):
        return (second, first) if kind == 0 else (first, second)

    def place(kind, first, second):
        dy, dx = step(kind, first, second)
        device, q, _ = at(dy, 0, dx)
        return device, q

    def send(q, low, count, c, sem, device):
        piece = win.at[pl.ds(q * NZ + low, count), part(c)]
        pltpu.make_async_remote_copy(
            src_ref=piece, dst_ref=piece, send_sem=xy_send.at[c], recv_sem=sem,
            device_id={"shot": device}).start()

    def arrive(q, low, count, c, sem):
        piece = win.at[pl.ds(q * NZ + low, count), part(c)]
        pltpu.make_async_copy(piece, piece, sem).wait()

    def spread(kind, hop, c):
        _, q = place(kind, hop, 0)
        for side, away in ((0, 1), (1, 3)):
            send(q, 2 * kind, 2, c, s2.at[c, kind, side, hop], place(kind, 0, away)[0])

    def stage_own(c):
        gathered(win, NZ - 1, zg_recv.at[c], c)
        for kind in range(2):
            _, q = place(kind, 0, 0)
            for side, away in ((0, 1), (1, 3)):
                send(q, 2 * kind, 2, c, s1.at[c, kind, side], place(kind, away, 0)[0])
        for kind in range(2):
            spread(kind, 0, c)

    def stage_near(c):
        for kind in range(2):
            for side, away in ((0, 1), (1, 3)):
                back = 4 - away
                _, q = place(kind, back, 0)
                arrive(q, 2 * kind, 2, c, s1.at[c, kind, side])
                send(q, 2 * kind + side, 1, c, f1.at[c, kind, side], place(kind, away, 0)[0])
                spread(kind, back, c)

    def stage_far(c):
        for kind in range(2):
            _, q = place(kind, 2, 0)
            for side in range(2):
                arrive(q, 2 * kind + side, 1, c, f1.at[c, kind, side])
            spread(kind, 2, c)

    hops = (0, 3, 1, 2)

    def stage_second(c):
        for hop in hops:
            for kind in range(2):
                for side, away in ((0, 1), (1, 3)):
                    back = 4 - away
                    _, q = place(kind, hop, back)
                    arrive(q, 2 * kind, 2, c, s2.at[c, kind, side, hop])
                    send(q, 2 * kind + side, 1, c, f2.at[c, kind, side, hop], place(kind, 0, away)[0])

    def stage_last(c):
        for hop in hops:
            for kind in range(2):
                _, q = place(kind, hop, 2)
                for side in range(2):
                    arrive(q, 2 * kind + side, 1, c, f2.at[c, kind, side, hop])

    def compute(c):
        acc[...] = jnp.zeros_like(acc)

        def body(q, carry):
            tiles = [win[q * NZ + h, part(c)] for h in range(4)]
            lhs = jnp.concatenate(
                [jnp.concatenate([x[:, b * TAPS:(b + 1) * TAPS] for x in tiles], axis=1) for b in range(4)], axis=0)
            start = pl.multiple_of(q * (4 * TAPS), 4 * TAPS)
            acc[...] += jnp.dot(lhs, band[pl.ds(start, 4 * TAPS), :], preferred_element_type=jnp.float32)
            return carry

        lax.fori_loop(0, PLANE, body, 0)
        lane = lax.broadcasted_iota(jnp.int32, (size, LANES), 1)
        for s in range(shots):
            cols = slice(s * LANES, (s + 1) * LANES)
            a = [acc[b * size:(b + 1) * size, cols] for b in range(4)]
            odd, last = pltpu.roll(a[1], TAPS, 1), pltpu.roll(a[3], TAPS, 1)
            low = a[0] + jnp.where(lane >= TAPS, odd, 0.0)
            high = a[2] + jnp.where(lane < TAPS, odd, last)
            for half, value in ((0, low), (1, high)):
                span = slice(half * LANES, (half + 1) * LANES)
                out[s, part(c), span] = (data[s, part(c), span].astype(jnp.float32) - value).astype(jnp.bfloat16)

    last = CHUNKS - 1
    stage_plane(0)
    stage_column(0)
    stage_plane(1)
    stage_own(0)
    stage_column(1)
    stage_near(0)
    stage_plane(2)
    stage_own(1)
    stage_far(0)
    stage_column(2)
    stage_near(1)
    stage_second(0)
    stage_plane(3)
    stage_own(2)
    stage_far(1)
    stage_column(3)
    stage_near(2)
    stage_last(0)
    stage_second(1)
    stage_own(3)
    stage_far(2)
    compute(0)
    stage_near(3)
    stage_last(1)
    stage_second(2)
    stage_far(3)
    compute(1)
    stage_last(2)
    stage_second(3)
    compute(2)
    stage_last(3)
    compute(3)

    for dr in range(1, NR):
        pltpu.make_async_copy(prim_in, prim.at[0], pr_send.at[dr]).wait()
    for c in range(CHUNKS):
        gathered(win, PLANE - 1, pa_send.at[c], c)
        gathered(win, NZ - 1, pb_send.at[c], c)
        gathered(win, NZ - 1, zg_send.at[c], c)
        gathered(win, 60, xy_send.at[c], c)


def shards(data, surface_traces, primaries, panel_owner):
    shots, rows, length = data.shape
    points = surface_traces.shape[0]
    size = rows // CHUNKS
    dma = pltpu.SemaphoreType.DMA
    vmem = pl.BlockSpec(memory_space=pltpu.VMEM)
    return pl.pallas_call(
        kernel,
        out_shape=jax.ShapeDtypeStruct(data.shape, jnp.bfloat16),
        in_specs=[pl.BlockSpec(memory_space=pltpu.SMEM), pl.BlockSpec(memory_space=pl.ANY), vmem, vmem],
        out_specs=vmem,
        scratch_shapes=[
            [pltpu.VMEM((PLANE, size, length), jnp.bfloat16)] * CHUNKS,
            pltpu.VMEM((NZ, rows, length), jnp.bfloat16),
            [pltpu.VMEM((NZ, size, length), jnp.bfloat16)] * CHUNKS,
            pltpu.VMEM((PLANE * NZ, rows, length), jnp.bfloat16),
            pltpu.VMEM((NR,) + primaries.shape, jnp.bfloat16),
            pltpu.VMEM((NR, shots, points, LANES), jnp.float32),
            pltpu.VMEM((PLANE * 4 * TAPS, shots * LANES), jnp.bfloat16),
            pltpu.VMEM((4 * size, shots * LANES), jnp.float32),
            dma((CHUNKS,)), dma((CHUNKS,)), dma((CHUNKS,)), dma((CHUNKS,)), dma((CHUNKS,)), dma((CHUNKS,)), dma((CHUNKS,)),
            dma, dma((NR,)), dma((NR,)),
            dma((CHUNKS,)), dma((CHUNKS, 2, 2)), dma((CHUNKS, 2, 2)), dma((CHUNKS, 2, 2, 4)), dma((CHUNKS, 2, 2, 4)),
        ],
        compiler_params=pltpu.CompilerParams(
            collective_id=0, has_side_effects=True, vmem_limit_bytes=60 * 1024 * 1024),
    )(panel_owner, surface_traces, primaries, data)


def solution(mesh):
    placed = (P("shot", "rcv", None), P("shot", "rcv", None), P("shot", "rcv", None), P())
    return jax.shard_map(
        shards, mesh=mesh, in_specs=placed, out_specs=P("shot", "rcv", None), check_vma=False
    )
```

time: 855 us -> 95.4 us (0.11)
  waiting for transfers between devices: 701 us -> 0 us
  Pallas kernels: 0 us -> 91.5 us
  local copies, waits for them, and re-layouts: 69.6 us -> 2.06 us
  matrix products: 43.1 us -> 0 us
  between operations: 16.3 us -> 0.01 us
  blocking collectives: 12.9 us -> 0 us
    psum x1 -> x0, waiting for transfers between devices: 701 us -> none  [broadcast(): return lax.psum(jnp.where(mine, value, jnp.zeros_like(value)), axis)]
    pallas_call x0 -> x1, Pallas kernels: none -> 91.5 us  [shards(): pl.pallas_call(kernel, out_shape=jax.ShapeDtypeStruct(data.shape, jnp.bfl...]
    dot_general x8 -> x0, matrix products: 43.1 us -> none  [the longest x4 25.5 us: band_matrices(): jnp.einsum('skt,ltio->lskio', panel_prim, shift_ones, preferred_element_t...]
    dot_general x4 -> x0, local copies, waits for them, and re-layouts: 36.8 us -> none  [band_matrices(): jnp.einsum('skt,ltio->lskio', panel_prim, shift_ones, preferred_element_t...]
    another operation x8 -> x0, local copies, waits for them, and re-layouts: 23 us -> none  [convolve(): stacked = jnp.stack([blocks, earlier])]
    psum x1 -> x0, blocking collectives: 12.9 us -> none  [broadcast(): return lax.psum(jnp.where(mine, value, jnp.zeros_like(value)), axis)]
  transfers between devices with their start and end apart: 1 -> 0, of which waited for: 1 -> 0; matrix products, arithmetic and copies ran while one was open for 8% -> 0% of each run, Pallas kernels for 0% -> 0%
where the time goes in v1:
time: 95.4 us; the launch traced here: 93.6 us
  Pallas kernels  91.5 us (96%)
  local copies, waits for them, and re-layouts  2.06 us (2%)
    pallas_call x1, Pallas kernels, shards(): pl.pallas_call(kernel, out_shape=jax.ShapeDtypeStruct(data.shape, jnp.bfl...  91.5 us
    unnamed x1, local copies, waits for them, and re-layouts  2.06 us

profile of v1, /device:TPU:2, one launch (start us, length us, event | category | flops | bytes accessed | tf_op | source)
XLA Modules:
  0.0 93.6 jit_solution(9235672894764121855)
XLA Ops:
  0.0 91.5 %shard_map.46 = bf16[6,256,256]{2,1,0:T(8,128)(2,1)} custom-call(s32[4]{0:T(128)} %owner.1, bf16[16,256,256]{2,1,0:T(8,128)(2,1)} %traces.1, bf16[6,16,64]{2,1,0:T(8,128)(2,1)} %prim_in.1, bf16[6,256,256]{2,1,0:T(8,128)(2,1)} %data.1), custom_call_target="tpu_custom_call" | custom-call | tf_op jit(solution)/shard_map/pallas_call | solution.py:255
  91.5 2.1 %copy.6 = bf16[6,256,256]{2,1,0:T(8,128)(2,1)} copy(bf16[6,256,256]{2,1,0:T(8,128)(2,1)} %shard_map.46) | data formatting | bytes 1572864

commit v2 on v0

v2 whole, which is shorter than its diff:
```python
import jax
import jax.numpy as jnp
from jax import lax
from jax.experimental import pallas as pl
from jax.experimental.pallas import tpu as pltpu
from jax.sharding import PartitionSpec as P

NY, NZ, NX = 4, 4, 4
NR = 4
PLANE = NY * NX
TAPS = 64
LANES = 128
CHUNKS = 4


def kernel(owner, traces, prim_in, data, out, ra, sb, rb, win, prim, prim32, band, lhs, acc, held, res,
           own_sem, pa_send, pa_recv, pb_send, pb_recv, zg_send, zg_recv,
           px_own, px_send, px_recv, pr_send, pr_recv, y_send, y1, y2, d_own, d_send, d_recv, o_own, o_send, o_recv):
    shots, rows, length = data.shape
    size = rows // NX
    wide = shots * LANES
    deep = NY * 4 * TAPS
    shot = lax.axis_index("shot")
    rcv = lax.axis_index("rcv")
    my_x = lax.rem(shot, NX)
    my_z = lax.rem(shot // NX, NZ)
    my_y = shot // (NX * NZ)
    my_q = my_y * NX + my_x

    def at(dy, dz, dx):
        y = lax.rem(my_y + dy, NY)
        z = lax.rem(my_z + dz, NZ)
        x = lax.rem(my_x + dx, NX)
        return (y * NZ + z) * NX + x, y, z, x

    def part(x):
        return pl.ds(pl.multiple_of(x * size, size), size)

    plane = [(dy, dx) for dy in range(NY) for dx in range(NX) if dy or dx]
    order = sorted(plane, key=lambda d: -(min(d[0], NY - d[0]) + min(d[1], NX - d[1])))

    barrier = pltpu.get_barrier_semaphore()
    for dy, dx in plane:
        pl.semaphore_signal(barrier, inc=1, device_id={"shot": at(dy, 0, dx)[0]})
    for dz in range(1, NZ):
        pl.semaphore_signal(barrier, inc=1, device_id={"shot": at(0, dz, 0)[0]})
    for dr in range(1, NR):
        pl.semaphore_signal(barrier, inc=1, device_id={"rcv": lax.rem(rcv + dr, NR)})
    pltpu.make_async_copy(prim_in, prim.at[rcv, my_x], px_own).start()
    for c in range(CHUNKS):
        pltpu.make_async_copy(traces.at[my_y * 4 + c, part(my_x)], ra[c].at[my_q], own_sem.at[c]).start()
    pltpu.make_async_copy(data.at[:, part(my_x)], held.at[my_x], d_own).start()
    pl.semaphore_wait(barrier, len(plane) + NZ - 1 + NR - 1)

    for dx in range(1, NX):
        pltpu.make_async_remote_copy(
            src_ref=prim_in, dst_ref=prim.at[rcv, my_x], send_sem=px_send.at[dx], recv_sem=px_recv.at[dx],
            device_id={"shot": at(0, 0, dx)[0]}).start()

    for c in range(CHUNKS):
        for dy, dx in order:
            device, y, _, x = at(dy, 0, dx)
            pltpu.make_async_remote_copy(
                src_ref=traces.at[y * 4 + c, part(x)], dst_ref=ra[c].at[my_q],
                send_sem=pa_send.at[c], recv_sem=pa_recv.at[c], device_id={"shot": device}).start()

    for dx in (2, 1, 3):
        device, _, _, x = at(0, 0, dx)
        pltpu.make_async_remote_copy(
            src_ref=data.at[:, part(x)], dst_ref=held.at[my_x], send_sem=d_send.at[dx], recv_sem=d_recv.at[dx],
            device_id={"shot": device}).start()

    def responses_x():
        pltpu.make_async_copy(prim_in, prim.at[rcv, my_x], px_own).wait()
        for dx in range(1, NX):
            pltpu.make_async_copy(prim_in, prim.at[rcv, my_x], px_recv.at[dx]).wait()
        for dr in range(1, NR):
            pltpu.make_async_remote_copy(
                src_ref=prim.at[rcv], dst_ref=prim.at[rcv], send_sem=pr_send.at[dr], recv_sem=pr_recv.at[dr],
                device_id={"rcv": lax.rem(rcv + dr, NR)}).start()

    def responses_rcv():
        for dr in range(1, NR):
            pltpu.make_async_copy(prim.at[0], prim.at[0], pr_recv.at[dr]).wait()
        prim32[...] = jnp.zeros_like(prim32)
        prim32[:, :, :, :, 0:TAPS] = prim[...].astype(jnp.float32)

    def make_bands(c):
        def body(step, carry):
            x, y = step // NY, lax.rem(step, NY)
            for h in range(4):
                for s in range(shots):
                    row = prim32[h, x, s, pl.ds(y * 4 + c, 1), :]
                    tile = pltpu.roll(jnp.broadcast_to(row, (TAPS, LANES)), 0, 1, stride=1, stride_axis=0)
                    start = pl.multiple_of(c * deep + y * (4 * TAPS) + h * TAPS, TAPS)
                    band[x, pl.ds(start, TAPS), s * LANES:(s + 1) * LANES] = tile.astype(jnp.bfloat16)
            return carry

        lax.fori_loop(0, NX * NY, body, 0)

    def gathered(count, sem):
        piece = win.at[pl.ds(0, count)]
        pltpu.make_async_copy(piece, piece, sem).wait()

    def split(index):
        return index // (NX * NZ) * NX + lax.rem(index, NX), lax.rem(index // NX, NZ)

    def stage_plane(c):
        pltpu.make_async_copy(traces.at[0, part(0)], ra[c].at[0], own_sem.at[c]).wait()
        gathered(PLANE - 1, pa_recv.at[c])
        for h in range(NZ):
            sb[c, h] = ra[c][split(owner[h])[0]]
        for dz in range(1, NZ):
            device, _, z, _ = at(0, dz, 0)
            pltpu.make_async_remote_copy(
                src_ref=sb.at[c, z], dst_ref=rb[c].at[my_z],
                send_sem=pb_send.at[c], recv_sem=pb_recv.at[c], device_id={"shot": device}).start()
        rb[c][my_z] = sb[c, my_z]

    def unit(y, c):
        return (y * 4 + c) * NZ

    def stage_column(c):
        gathered(NZ - 1, pb_recv.at[c])
        mine = unit(my_y, c) + my_z
        win[mine] = rb[c][split(owner[my_z])[1]]
        for dz in range(1, NZ):
            device = at(0, dz, 0)[0]
            pltpu.make_async_remote_copy(
                src_ref=win.at[mine], dst_ref=win.at[mine],
                send_sem=zg_send.at[c], recv_sem=zg_recv.at[c], device_id={"shot": device}).start()

    def send_y(y, low, count, c, sem, away):
        piece = win.at[pl.ds(unit(y, c) + low, count)]
        pltpu.make_async_remote_copy(
            src_ref=piece, dst_ref=piece, send_sem=y_send.at[c], recv_sem=sem,
            device_id={"shot": at(away, 0, 0)[0]}).start()

    def arrive_y(y, low, count, c, sem):
        piece = win.at[pl.ds(unit(y, c) + low, count)]
        pltpu.make_async_copy(piece, piece, sem).wait()

    sides = ((0, 1), (1, 3))

    def stage_own(c):
        gathered(NZ - 1, zg_recv.at[c])
        for side, away in sides:
            send_y(my_y, 0, 4, c, y1.at[c, side], away)

    def stage_near(c):
        for side, away in sides:
            y = at(4 - away, 0, 0)[1]
            arrive_y(y, 0, 4, c, y1.at[c, side])
            send_y(y, 2 * side, 2, c, y2.at[c, side], away)

    def stage_far(c):
        y = at(2, 0, 0)[1]
        for side, _ in sides:
            arrive_y(y, 2 * side, 2, c, y2.at[c, side])

    def stack(c):
        for y in range(NY):
            tiles = [win[unit(y, c) + h] for h in range(4)]
            for b in range(4):
                lhs[b * size:(b + 1) * size, y * 4 * TAPS:(y + 1) * 4 * TAPS] = jnp.concatenate(
                    [t[:, b * TAPS:(b + 1) * TAPS] for t in tiles], axis=1)

    def product(x, c):
        return jnp.dot(lhs[...], band[x, c * deep:(c + 1) * deep, :], preferred_element_type=jnp.float32)

    def compute(c):
        stack(c)

        def body(x, carry):
            if c == 0:
                acc[x] = product(x, c)
            else:
                acc[x] += product(x, c)
            return carry

        lax.fori_loop(0, NX, body, 0)

    def finish(dx):
        device, _, _, x = at(0, 0, dx)
        acc[x] += product(x, CHUNKS - 1)
        lane = lax.broadcasted_iota(jnp.int32, (size, LANES), 1)
        for s in range(shots):
            a = [acc[x, b * size:(b + 1) * size, s * LANES:(s + 1) * LANES] for b in range(4)]
            odd, last = pltpu.roll(a[1], TAPS, 1), pltpu.roll(a[3], TAPS, 1)
            low = a[0] + jnp.where(lane >= TAPS, odd, 0.0)
            high = a[2] + jnp.where(lane < TAPS, odd, last)
            for half, value in ((0, low), (1, high)):
                span = slice(half * LANES, (half + 1) * LANES)
                res[x, s, :, span] = (held[x, s, :, span].astype(jnp.float32) - value).astype(jnp.bfloat16)
        if dx:
            pltpu.make_async_remote_copy(
                src_ref=res.at[x], dst_ref=out.at[:, part(my_x)], send_sem=o_send.at[dx], recv_sem=o_recv.at[dx],
                device_id={"shot": device}).start()
        else:
            pltpu.make_async_copy(res.at[x], out.at[:, part(my_x)], o_own).start()

    responses_x()
    stage_plane(0)
    responses_rcv()
    make_bands(0)
    stage_column(0)
    make_bands(1)
    stage_plane(1)
    stage_own(0)
    stage_column(1)
    make_bands(2)
    stage_plane(2)
    stage_near(0)
    stage_own(1)
    stage_column(2)
    stage_far(0)
    make_bands(3)
    stage_plane(3)
    stage_near(1)
    stage_own(2)
    stage_far(1)
    compute(0)
    stage_column(3)
    stage_near(2)
    compute(1)
    stage_own(3)
    stage_far(2)
    compute(2)
    stage_near(3)
    pltpu.make_async_copy(data.at[:, part(0)], held.at[0], d_own).wait()
    for dx in range(1, NX):
        pltpu.make_async_copy(data.at[:, part(0)], held.at[0], d_recv.at[dx]).wait()
    stage_far(3)
    stack(3)
    for dx in (2, 1, 3, 0):
        finish(dx)

    for dx in range(1, NX):
        pltpu.make_async_copy(prim_in, prim.at[0, 0], px_send.at[dx]).wait()
        pltpu.make_async_copy(data.at[:, part(0)], held.at[0], d_send.at[dx]).wait()
    for dr in range(1, NR):
        pltpu.make_async_copy(prim.at[0], prim.at[0], pr_send.at[dr]).wait()
    for c in range(CHUNKS):
        gathered(PLANE - 1, pa_send.at[c])
        gathered(NZ - 1, pb_send.at[c])
        gathered(NZ - 1, zg_send.at[c])
        gathered(12, y_send.at[c])
    pltpu.make_async_copy(res.at[0], out.at[:, part(0)], o_own).wait()
    for dx in range(1, NX):
        pltpu.make_async_copy(res.at[0], out.at[:, part(0)], o_send.at[dx]).wait()
        pltpu.make_async_copy(res.at[0], out.at[:, part(0)], o_recv.at[dx]).wait()


def shards(data, surface_traces, primaries, panel_owner):
    shots, rows, length = data.shape
    points = surface_traces.shape[0]
    size = rows // NX
    dma = pltpu.SemaphoreType.DMA
    anywhere = pl.BlockSpec(memory_space=pl.ANY)
    return pl.pallas_call(
        kernel,
        out_shape=jax.ShapeDtypeStruct(data.shape, jnp.bfloat16),
        in_specs=[pl.BlockSpec(memory_space=pltpu.SMEM), anywhere, pl.BlockSpec(memory_space=pltpu.VMEM), anywhere],
        out_specs=anywhere,
        scratch_shapes=[
            [pltpu.VMEM((PLANE, size, length), jnp.bfloat16)] * CHUNKS,
            pltpu.VMEM((CHUNKS, NZ, size, length), jnp.bfloat16),
            [pltpu.VMEM((NZ, size, length), jnp.bfloat16)] * CHUNKS,
            pltpu.VMEM((PLANE * NZ, size, length), jnp.bfloat16),
            pltpu.VMEM((NR, NX) + primaries.shape, jnp.bfloat16),
            pltpu.VMEM((NR, NX, shots, points, LANES), jnp.float32),
            pltpu.VMEM((NX, PLANE * 4 * TAPS, shots * LANES), jnp.bfloat16),
            pltpu.VMEM((4 * size, NY * 4 * TAPS), jnp.bfloat16),
            pltpu.VMEM((NX, 4 * size, shots * LANES), jnp.float32),
            pltpu.VMEM((NX, shots, size, length), jnp.bfloat16),
            pltpu.VMEM((NX, shots, size, length), jnp.bfloat16),
            dma((CHUNKS,)), dma((CHUNKS,)), dma((CHUNKS,)), dma((CHUNKS,)), dma((CHUNKS,)), dma((CHUNKS,)), dma((CHUNKS,)),
            dma, dma((NX,)), dma((NX,)), dma((NR,)), dma((NR,)),
            dma((CHUNKS,)), dma((CHUNKS, 2)), dma((CHUNKS, 2)),
            dma, dma((NX,)), dma((NX,)), dma, dma((NX,)), dma((NX,)),
        ],
        compiler_params=pltpu.CompilerParams(
            collective_id=0, has_side_effects=True, vmem_limit_bytes=60 * 1024 * 1024),
    )(panel_owner, surface_traces, primaries, data)


def solution(mesh):
    placed = (P("shot", "rcv", None), P("shot", "rcv", None), P("shot", "rcv", None), P())
    return jax.shard_map(
        shards, mesh=mesh, in_specs=placed, out_specs=P("shot", "rcv", None), check_vma=False
    )
```

time: 855 us -> 79.5 us (0.09)
  waiting for transfers between devices: 701 us -> 0 us
  Pallas kernels: 0 us -> 77.3 us
  local copies, waits for them, and re-layouts: 69.6 us -> 2.06 us
  matrix products: 43.1 us -> 0 us
  between operations: 16.3 us -> 0.01 us
  blocking collectives: 12.9 us -> 0 us
    psum x1 -> x0, waiting for transfers between devices: 701 us -> none  [broadcast(): return lax.psum(jnp.where(mine, value, jnp.zeros_like(value)), axis)]
    pallas_call x0 -> x1, Pallas kernels: none -> 77.3 us  [shards(): pl.pallas_call(kernel, out_shape=jax.ShapeDtypeStruct(data.shape, jnp.bfl...]
    dot_general x8 -> x0, matrix products: 43.1 us -> none  [the longest x4 25.5 us: band_matrices(): jnp.einsum('skt,ltio->lskio', panel_prim, shift_ones, preferred_element_t...]
    dot_general x4 -> x0, local copies, waits for them, and re-layouts: 36.8 us -> none  [band_matrices(): jnp.einsum('skt,ltio->lskio', panel_prim, shift_ones, preferred_element_t...]
    another operation x8 -> x0, local copies, waits for them, and re-layouts: 23 us -> none  [convolve(): stacked = jnp.stack([blocks, earlier])]
    psum x1 -> x0, blocking collectives: 12.9 us -> none  [broadcast(): return lax.psum(jnp.where(mine, value, jnp.zeros_like(value)), axis)]
  transfers between devices with their start and end apart: 1 -> 0, of which waited for: 1 -> 0; matrix products, arithmetic and copies ran while one was open for 8% -> 0% of each run, Pallas kernels for 0% -> 0%
where the time goes in v2:
time: 79.5 us; the launch traced here: 79.3 us
  Pallas kernels  77.3 us (97%)
  local copies, waits for them, and re-layouts  2.06 us (3%)
    pallas_call x1, Pallas kernels, shards(): pl.pallas_call(kernel, out_shape=jax.ShapeDtypeStruct(data.shape, jnp.bfl...  77.3 us
    unnamed x1, local copies, waits for them, and re-layouts  2.06 us

profile of v2, /device:TPU:2, one launch (start us, length us, event | category | flops | bytes accessed | tf_op | source)
XLA Modules:
  0.0 79.3 jit_solution(17618531236175238823)
XLA Ops:
  0.0 77.3 %shard_map.46 = bf16[6,256,256]{2,1,0:T(8,128)(2,1)} custom-call(s32[4]{0:T(128)} %owner.1, bf16[16,256,256]{2,1,0:T(8,128)(2,1)} %traces.1, bf16[6,16,64]{2,1,0:T(8,128)(2,1)} %prim_in.1, bf16[6,256,256]{2,1,0:T(8,128)(2,1)} %data.1), custom_call_target="tpu_custom_call" | custom-call | tf_op jit(solution)/shard_map/pallas_call | solution.py:260
  77.3 2.1 %copy.6 = bf16[6,256,256]{2,1,0:T(8,128)(2,1)} copy(bf16[6,256,256]{2,1,0:T(8,128)(2,1)} %shard_map.46) | data formatting | bytes 1572864

commit v3 on v2

--- a/solution.py
+++ b/solution.py
@@ -10,15 +10,17 @@
 PLANE = NY * NX
 TAPS = 64
 LANES = 128
-CHUNKS = 4
+HALVES = 2
+POINTS = 4
+CHUNKS = HALVES * POINTS
+COLUMN, OWN, NEAR, FAR = 2, 4, 6, 7
 
 
 def kernel(owner, traces, prim_in, data, out, ra, sb, rb, win, prim, prim32, band, lhs, acc, held, res,
            own_sem, pa_send, pa_recv, pb_send, pb_recv, zg_send, zg_recv,
            px_own, px_send, px_recv, pr_send, pr_recv, y_send, y1, y2, d_own, d_send, d_recv, o_own, o_send, o_recv):
     shots, rows, length = data.shape
-    size = rows // NX
-    wide = shots * LANES
+    size = rows // (NX * HALVES)
     deep = NY * 4 * TAPS
     shot = lax.axis_index("shot")
     rcv = lax.axis_index("rcv")
@@ -33,8 +35,8 @@
         x = lax.rem(my_x + dx, NX)
         return (y * NZ + z) * NX + x, y, z, x
 
-    def part(x):
-        return pl.ds(pl.multiple_of(x * size, size), size)
+    def part(x, half):
+        return pl.ds(pl.multiple_of(x * (size * HALVES) + half * size, size), size)
 
     plane = [(dy, dx) for dy in range(NY) for dx in range(NX) if dy or dx]
     order = sorted(plane, key=lambda d: -(min(d[0], NY - d[0]) + min(d[1], NX - d[1])))
@@ -48,8 +50,10 @@
         pl.semaphore_signal(barrier, inc=1, device_id={"rcv": lax.rem(rcv + dr, NR)})
     pltpu.make_async_copy(prim_in, prim.at[rcv, my_x], px_own).start()
     for c in range(CHUNKS):
-        pltpu.make_async_copy(traces.at[my_y * 4 + c, part(my_x)], ra[c].at[my_q], own_sem.at[c]).start()
-    pltpu.make_async_copy(data.at[:, part(my_x)], held.at[my_x], d_own).start()
+        half, k = divmod(c, POINTS)
+        pltpu.make_async_copy(traces.at[my_y * POINTS + k, part(my_x, half)], ra[c].at[my_q], own_sem.at[c]).start()
+    for half in range(HALVES):
+        pltpu.make_async_copy(data.at[:, part(my_x, half)], held.at[half, my_x], d_own.at[half]).start()
     pl.semaphore_wait(barrier, len(plane) + NZ - 1 + NR - 1)
 
     for dx in range(1, NX):
@@ -58,17 +62,19 @@
             device_id={"shot": at(0, 0, dx)[0]}).start()
 
     for c in range(CHUNKS):
+        half, k = divmod(c, POINTS)
         for dy, dx in order:
             device, y, _, x = at(dy, 0, dx)
             pltpu.make_async_remote_copy(
-                src_ref=traces.at[y * 4 + c, part(x)], dst_ref=ra[c].at[my_q],
+                src_ref=traces.at[y * POINTS + k, part(x, half)], dst_ref=ra[c].at[my_q],
                 send_sem=pa_send.at[c], recv_sem=pa_recv.at[c], device_id={"shot": device}).start()
 
-    for dx in (2, 1, 3):
-        device, _, _, x = at(0, 0, dx)
-        pltpu.make_async_remote_copy(
-            src_ref=data.at[:, part(x)], dst_ref=held.at[my_x], send_sem=d_send.at[dx], recv_sem=d_recv.at[dx],
-            device_id={"shot": device}).start()
+    for half in range(HALVES):
+        for dx in (2, 1, 3):
+            device, _, _, x = at(0, 0, dx)
+            pltpu.make_async_remote_copy(
+                src_ref=data.at[:, part(x, half)], dst_ref=held.at[half, my_x],
+                send_sem=d_send.at[half, dx], recv_sem=d_recv.at[half, dx], device_id={"shot": device}).start()
 
     def responses_x():
         pltpu.make_async_copy(prim_in, prim.at[rcv, my_x], px_own).wait()
@@ -85,14 +91,14 @@
         prim32[...] = jnp.zeros_like(prim32)
         prim32[:, :, :, :, 0:TAPS] = prim[...].astype(jnp.float32)
 
-    def make_bands(c):
+    def make_bands(k):
         def body(step, carry):
             x, y = step // NY, lax.rem(step, NY)
             for h in range(4):
                 for s in range(shots):
-                    row = prim32[h, x, s, pl.ds(y * 4 + c, 1), :]
+                    row = prim32[h, x, s, pl.ds(y * POINTS + k, 1), :]
                     tile = pltpu.roll(jnp.broadcast_to(row, (TAPS, LANES)), 0, 1, stride=1, stride_axis=0)
-                    start = pl.multiple_of(c * deep + y * (4 * TAPS) + h * TAPS, TAPS)
+                    start = pl.multiple_of(k * deep + y * (4 * TAPS) + h * TAPS, TAPS)
                     band[x, pl.ds(start, TAPS), s * LANES:(s + 1) * LANES] = tile.astype(jnp.bfloat16)
             return carry
 
@@ -106,7 +112,7 @@
         return index // (NX * NZ) * NX + lax.rem(index, NX), lax.rem(index // NX, NZ)
 
     def stage_plane(c):
-        pltpu.make_async_copy(traces.at[0, part(0)], ra[c].at[0], own_sem.at[c]).wait()
+        pltpu.make_async_copy(traces.at[0, part(0, 0)], ra[c].at[0], own_sem.at[c]).wait()
         gathered(PLANE - 1, pa_recv.at[c])
         for h in range(NZ):
             sb[c, h] = ra[c][split(owner[h])[0]]
@@ -118,7 +124,8 @@
         rb[c][my_z] = sb[c, my_z]
 
     def unit(y, c):
-        return (y * 4 + c) * NZ
+        half, k = divmod(c, POINTS)
+        return ((half * NY + y) * POINTS + k) * NZ
 
     def stage_column(c):
         gathered(NZ - 1, pb_recv.at[c])
@@ -165,79 +172,66 @@
                 lhs[b * size:(b + 1) * size, y * 4 * TAPS:(y + 1) * 4 * TAPS] = jnp.concatenate(
                     [t[:, b * TAPS:(b + 1) * TAPS] for t in tiles], axis=1)
 
-    def product(x, c):
-        return jnp.dot(lhs[...], band[x, c * deep:(c + 1) * deep, :], preferred_element_type=jnp.float32)
+    def product(x, k):
+        return jnp.dot(lhs[...], band[x, k * deep:(k + 1) * deep, :], preferred_element_type=jnp.float32)
 
     def compute(c):
+        half, k = divmod(c, POINTS)
         stack(c)
+        if k == POINTS - 1:
+            for dx in range(NX):
+                if dx == 0:
+                    pltpu.make_async_copy(data.at[:, part(0, 0)], held.at[0, 0], d_own.at[half]).wait()
+                else:
+                    pltpu.make_async_copy(data.at[:, part(0, 0)], held.at[0, 0], d_recv.at[half, dx]).wait()
+            for dx in (2, 1, 3, 0):
+                finish(half, dx)
+            return
 
         def body(x, carry):
-            if c == 0:
-                acc[x] = product(x, c)
+            if k == 0:
+                acc[x] = product(x, k)
             else:
-                acc[x] += product(x, c)
+                acc[x] += product(x, k)
             return carry
 
         lax.fori_loop(0, NX, body, 0)
 
-    def finish(dx):
+    def finish(half, dx):
         device, _, _, x = at(0, 0, dx)
-        acc[x] += product(x, CHUNKS - 1)
+        acc[x] += product(x, POINTS - 1)
         lane = lax.broadcasted_iota(jnp.int32, (size, LANES), 1)
         for s in range(shots):
             a = [acc[x, b * size:(b + 1) * size, s * LANES:(s + 1) * LANES] for b in range(4)]
             odd, last = pltpu.roll(a[1], TAPS, 1), pltpu.roll(a[3], TAPS, 1)
             low = a[0] + jnp.where(lane >= TAPS, odd, 0.0)
             high = a[2] + jnp.where(lane < TAPS, odd, last)
-            for half, value in ((0, low), (1, high)):
-                span = slice(half * LANES, (half + 1) * LANES)
-                res[x, s, :, span] = (held[x, s, :, span].astype(jnp.float32) - value).astype(jnp.bfloat16)
+            for side, value in ((0, low), (1, high)):
+                span = slice(side * LANES, (side + 1) * LANES)
+                res[half, x, s, :, span] = (held[half, x, s, :, span].astype(jnp.float32) - value).astype(jnp.bfloat16)
         if dx:
             pltpu.make_async_remote_copy(
-                src_ref=res.at[x], dst_ref=out.at[:, part(my_x)], send_sem=o_send.at[dx], recv_sem=o_recv.at[dx],
-                device_id={"shot": device}).start()
+                src_ref=res.at[half, x], dst_ref=out.at[:, part(my_x, half)],
+                send_sem=o_send.at[half, dx], recv_sem=o_recv.at[half, dx], device_id={"shot": device}).start()
         else:
-            pltpu.make_async_copy(res.at[x], out.at[:, part(my_x)], o_own).start()
+            pltpu.make_async_copy(res.at[half, x], out.at[:, part(my_x, half)], o_own.at[half]).start()
 
     responses_x()
-    stage_plane(0)
-    responses_rcv()
-    make_bands(0)
-    stage_column(0)
-    make_bands(1)
-    stage_plane(1)
-    stage_own(0)
-    stage_column(1)
-    make_bands(2)
-    stage_plane(2)
-    stage_near(0)
-    stage_own(1)
-    stage_column(2)
-    stage_far(0)
-    make_bands(3)
-    stage_plane(3)
-    stage_near(1)
-    stage_own(2)
-    stage_far(1)
-    compute(0)
-    stage_column(3)
-    stage_near(2)
-    compute(1)
-    stage_own(3)
-    stage_far(2)
-    compute(2)
-    stage_near(3)
-    pltpu.make_async_copy(data.at[:, part(0)], held.at[0], d_own).wait()
-    for dx in range(1, NX):
-        pltpu.make_async_copy(data.at[:, part(0)], held.at[0], d_recv.at[dx]).wait()
-    stage_far(3)
-    stack(3)
-    for dx in (2, 1, 3, 0):
-        finish(dx)
+    for slot in range(CHUNKS + FAR):
+        for behind, stage in ((FAR, stage_far), (NEAR, stage_near), (OWN, stage_own), (COLUMN, stage_column), (0, stage_plane)):
+            if 0 <= slot - behind < CHUNKS:
+                stage(slot - behind)
+        if slot == 0:
+            responses_rcv()
+        if 1 <= slot <= POINTS:
+            make_bands(slot - 1)
+        if slot >= FAR:
+            compute(slot - FAR)
 
     for dx in range(1, NX):
         pltpu.make_async_copy(prim_in, prim.at[0, 0], px_send.at[dx]).wait()
-        pltpu.make_async_copy(data.at[:, part(0)], held.at[0], d_send.at[dx]).wait()
+        for half in range(HALVES):
+            pltpu.make_async_copy(data.at[:, part(0, 0)], held.at[0, 0], d_send.at[half, dx]).wait()
     for dr in range(1, NR):
         pltpu.make_async_copy(prim.at[0], prim.at[0], pr_send.at[dr]).wait()
     for c in range(CHUNKS):
@@ -245,16 +239,17 @@
         gathered(NZ - 1, pb_send.at[c])
         gathered(NZ - 1, zg_send.at[c])
         gathered(12, y_send.at[c])
-    pltpu.make_async_copy(res.at[0], out.at[:, part(0)], o_own).wait()
-    for dx in range(1, NX):
-        pltpu.make_async_copy(res.at[0], out.at[:, part(0)], o_send.at[dx]).wait()
-        pltpu.make_async_copy(res.at[0], out.at[:, part(0)], o_recv.at[dx]).wait()
+    for half in range(HALVES):
+        pltpu.make_async_copy(res.at[0, 0], out.at[:, part(0, 0)], o_own.at[half]).wait()
+        for dx in range(1, NX):
+            pltpu.make_async_copy(res.at[0, 0], out.at[:, part(0, 0)], o_send.at[half, dx]).wait()
+            pltpu.make_async_copy(res.at[0, 0], out.at[:, part(0, 0)], o_recv.at[half, dx]).wait()
 
 
 def shards(data, surface_traces, primaries, panel_owner):
     shots, rows, length = data.shape
     points = surface_traces.shape[0]
-    size = rows // NX
+    size = rows // (NX * HALVES)
     dma = pltpu.SemaphoreType.DMA
     anywhere = pl.BlockSpec(memory_space=pl.ANY)
     return pl.pallas_call(
@@ -266,18 +261,18 @@
             [pltpu.VMEM((PLANE, size, length), jnp.bfloat16)] * CHUNKS,
             pltpu.VMEM((CHUNKS, NZ, size, length), jnp.bfloat16),
             [pltpu.VMEM((NZ, size, length), jnp.bfloat16)] * CHUNKS,
-            pltpu.VMEM((PLANE * NZ, size, length), jnp.bfloat16),
+            pltpu.VMEM((HALVES * PLANE * NZ, size, length), jnp.bfloat16),
             pltpu.VMEM((NR, NX) + primaries.shape, jnp.bfloat16),
             pltpu.VMEM((NR, NX, shots, points, LANES), jnp.float32),
             pltpu.VMEM((NX, PLANE * 4 * TAPS, shots * LANES), jnp.bfloat16),
             pltpu.VMEM((4 * size, NY * 4 * TAPS), jnp.bfloat16),
             pltpu.VMEM((NX, 4 * size, shots * LANES), jnp.float32),
-            pltpu.VMEM((NX, shots, size, length), jnp.bfloat16),
-            pltpu.VMEM((NX, shots, size, length), jnp.bfloat16),
+            pltpu.VMEM((HALVES, NX, shots, size, length), jnp.bfloat16),
+            pltpu.VMEM((HALVES, NX, shots, size, length), jnp.bfloat16),
             dma((CHUNKS,)), dma((CHUNKS,)), dma((CHUNKS,)), dma((CHUNKS,)), dma((CHUNKS,)), dma((CHUNKS,)), dma((CHUNKS,)),
             dma, dma((NX,)), dma((NX,)), dma((NR,)), dma((NR,)),
             dma((CHUNKS,)), dma((CHUNKS, 2)), dma((CHUNKS, 2)),
-            dma, dma((NX,)), dma((NX,)), dma, dma((NX,)), dma((NX,)),
+            dma((HALVES,)), dma((HALVES, NX)), dma((HALVES, NX)), dma((HALVES,)), dma((HALVES, NX)), dma((HALVES, NX)),
         ],
         compiler_params=pltpu.CompilerParams(
             collective_id=0, has_side_effects=True, vmem_limit_bytes=60 * 1024 * 1024),

time: 79.5 us -> 75 us (0.943)
  Pallas kernels: 77.3 us -> 72.7 us
    pallas_call x1, Pallas kernels: 77.3 us -> 72.7 us  [shards(): pl.pallas_call(kernel, out_shape=jax.ShapeDtypeStruct(data.shape, jnp.bfl...]
where the time goes in v3:
time: 75 us; the launch traced here: 74.8 us
  Pallas kernels  72.7 us (97%)
  local copies, waits for them, and re-layouts  2.06 us (3%)
    pallas_call x1, Pallas kernels, shards(): pl.pallas_call(kernel, out_shape=jax.ShapeDtypeStruct(data.shape, jnp.bfl...  72.7 us
    unnamed x1, local copies, waits for them, and re-layouts  2.06 us

profile of v3, /device:TPU:2, one launch (start us, length us, event | category | flops | bytes accessed | tf_op | source)
XLA Modules:
  0.0 74.8 jit_solution(16800372777424726993)
XLA Ops:
  0.0 72.7 %shard_map.46 = bf16[6,256,256]{2,1,0:T(8,128)(2,1)} custom-call(s32[4]{0:T(128)} %owner.1, bf16[16,256,256]{2,1,0:T(8,128)(2,1)} %traces.1, bf16[6,16,64]{2,1,0:T(8,128)(2,1)} %prim_in.1, bf16[6,256,256]{2,1,0:T(8,128)(2,1)} %data.1), custom_call_target="tpu_custom_call" | custom-call | tf_op jit(solution)/shard_map/pallas_call | solution.py:255
  72.7 2.1 %copy.6 = bf16[6,256,256]{2,1,0:T(8,128)(2,1)} copy(bf16[6,256,256]{2,1,0:T(8,128)(2,1)} %shard_map.46) | data formatting | bytes 1572864

commit v4 on v3

--- a/solution.py
+++ b/solution.py
@@ -11,9 +11,10 @@
 TAPS = 64
 LANES = 128
 HALVES = 2
-POINTS = 4
+GROUP = 2
+POINTS = 4 // GROUP
 CHUNKS = HALVES * POINTS
-COLUMN, OWN, NEAR, FAR = 2, 4, 6, 7
+COLUMN, OWN, NEAR, FAR = 2, 3, 4, 5
 
 
 def kernel(owner, traces, prim_in, data, out, ra, sb, rb, win, prim, prim32, band, lhs, acc, held, res,
@@ -51,7 +52,7 @@
     pltpu.make_async_copy(prim_in, prim.at[rcv, my_x], px_own).start()
     for c in range(CHUNKS):
         half, k = divmod(c, POINTS)
-        pltpu.make_async_copy(traces.at[my_y * POINTS + k, part(my_x, half)], ra[c].at[my_q], own_sem.at[c]).start()
+        pltpu.make_async_copy(traces.at[pl.ds(my_y * 4 + k * GROUP, GROUP), part(my_x, half)], ra[c].at[my_q], own_sem.at[c]).start()
     for half in range(HALVES):
         pltpu.make_async_copy(data.at[:, part(my_x, half)], held.at[half, my_x], d_own.at[half]).start()
     pl.semaphore_wait(barrier, len(plane) + NZ - 1 + NR - 1)
@@ -66,7 +67,7 @@
         for dy, dx in order:
             device, y, _, x = at(dy, 0, dx)
             pltpu.make_async_remote_copy(
-                src_ref=traces.at[y * POINTS + k, part(x, half)], dst_ref=ra[c].at[my_q],
+                src_ref=traces.at[pl.ds(y * 4 + k * GROUP, GROUP), part(x, half)], dst_ref=ra[c].at[my_q],
                 send_sem=pa_send.at[c], recv_sem=pa_recv.at[c], device_id={"shot": device}).start()
 
     for half in range(HALVES):
@@ -96,7 +97,7 @@
             x, y = step // NY, lax.rem(step, NY)
             for h in range(4):
                 for s in range(shots):
-                    row = prim32[h, x, s, pl.ds(y * POINTS + k, 1), :]
+                    row = prim32[h, x, s, pl.ds(y * 4 + k, 1), :]
                     tile = pltpu.roll(jnp.broadcast_to(row, (TAPS, LANES)), 0, 1, stride=1, stride_axis=0)
                     start = pl.multiple_of(k * deep + y * (4 * TAPS) + h * TAPS, TAPS)
                     band[x, pl.ds(start, TAPS), s * LANES:(s + 1) * LANES] = tile.astype(jnp.bfloat16)
@@ -112,7 +113,7 @@
         return index // (NX * NZ) * NX + lax.rem(index, NX), lax.rem(index // NX, NZ)
 
     def stage_plane(c):
-        pltpu.make_async_copy(traces.at[0, part(0, 0)], ra[c].at[0], own_sem.at[c]).wait()
+        pltpu.make_async_copy(traces.at[pl.ds(0, GROUP), part(0, 0)], ra[c].at[0], own_sem.at[c]).wait()
         gathered(PLANE - 1, pa_recv.at[c])
         for h in range(NZ):
             sb[c, h] = ra[c][split(owner[h])[0]]
@@ -167,13 +168,15 @@
 
     def stack(c):
         for y in range(NY):
-            tiles = [win[unit(y, c) + h] for h in range(4)]
-            for b in range(4):
-                lhs[b * size:(b + 1) * size, y * 4 * TAPS:(y + 1) * 4 * TAPS] = jnp.concatenate(
-                    [t[:, b * TAPS:(b + 1) * TAPS] for t in tiles], axis=1)
+            for i in range(GROUP):
+                tiles = [win[unit(y, c) + h, i] for h in range(4)]
+                start = i * deep + y * 4 * TAPS
+                for b in range(4):
+                    lhs[b * size:(b + 1) * size, start:start + 4 * TAPS] = jnp.concatenate(
+                        [t[:, b * TAPS:(b + 1) * TAPS] for t in tiles], axis=1)
 
     def product(x, k):
-        return jnp.dot(lhs[...], band[x, k * deep:(k + 1) * deep, :], preferred_element_type=jnp.float32)
+        return jnp.dot(lhs[...], band[x, k * GROUP * deep:(k + 1) * GROUP * deep, :], preferred_element_type=jnp.float32)
 
     def compute(c):
         half, k = divmod(c, POINTS)
@@ -223,7 +226,7 @@
                 stage(slot - behind)
         if slot == 0:
             responses_rcv()
-        if 1 <= slot <= POINTS:
+        if 1 <= slot <= 4:
             make_bands(slot - 1)
         if slot >= FAR:
             compute(slot - FAR)
@@ -258,14 +261,14 @@
         in_specs=[pl.BlockSpec(memory_space=pltpu.SMEM), anywhere, pl.BlockSpec(memory_space=pltpu.VMEM), anywhere],
         out_specs=anywhere,
         scratch_shapes=[
-            [pltpu.VMEM((PLANE, size, length), jnp.bfloat16)] * CHUNKS,
-            pltpu.VMEM((CHUNKS, NZ, size, length), jnp.bfloat16),
-            [pltpu.VMEM((NZ, size, length), jnp.bfloat16)] * CHUNKS,
-            pltpu.VMEM((HALVES * PLANE * NZ, size, length), jnp.bfloat16),
+            [pltpu.VMEM((PLANE, GROUP, size, length), jnp.bfloat16)] * CHUNKS,
+            pltpu.VMEM((CHUNKS, NZ, GROUP, size, length), jnp.bfloat16),
+            [pltpu.VMEM((NZ, GROUP, size, length), jnp.bfloat16)] * CHUNKS,
+            pltpu.VMEM((HALVES * NY * POINTS * NZ, GROUP, size, length), jnp.bfloat16),
             pltpu.VMEM((NR, NX) + primaries.shape, jnp.bfloat16),
             pltpu.VMEM((NR, NX, shots, points, LANES), jnp.float32),
             pltpu.VMEM((NX, PLANE * 4 * TAPS, shots * LANES), jnp.bfloat16),
-            pltpu.VMEM((4 * size, NY * 4 * TAPS), jnp.bfloat16),
+            pltpu.VMEM((4 * size, GROUP * NY * 4 * TAPS), jnp.bfloat16),
             pltpu.VMEM((NX, 4 * size, shots * LANES), jnp.float32),
             pltpu.VMEM((HALVES, NX, shots, size, length), jnp.bfloat16),
             pltpu.VMEM((HALVES, NX, shots, size, length), jnp.bfloat16),

time: 75 us -> 72.3 us (0.964)
  Pallas kernels: 72.7 us -> 69.5 us
    pallas_call x1, Pallas kernels: 72.7 us -> 69.5 us  [shards(): pl.pallas_call(kernel, out_shape=jax.ShapeDtypeStruct(data.shape, jnp.bfl...]
where the time goes in v4:
time: 72.3 us; the launch traced here: 71.6 us
  Pallas kernels  69.5 us (96%)
  local copies, waits for them, and re-layouts  2.06 us (3%)
    pallas_call x1, Pallas kernels, shards(): pl.pallas_call(kernel, out_shape=jax.ShapeDtypeStruct(data.shape, jnp.bfl...  69.5 us
    unnamed x1, local copies, waits for them, and re-layouts  2.06 us

profile of v4, /device:TPU:2, one launch (start us, length us, event | category | flops | bytes accessed | tf_op | source)
XLA Modules:
  0.0 71.6 jit_solution(3115068502578668986)
XLA Ops:
  0.0 69.5 %shard_map.46 = bf16[6,256,256]{2,1,0:T(8,128)(2,1)} custom-call(s32[4]{0:T(128)} %owner.1, bf16[16,256,256]{2,1,0:T(8,128)(2,1)} %traces.1, bf16[6,16,64]{2,1,0:T(8,128)(2,1)} %prim_in.1, bf16[6,256,256]{2,1,0:T(8,128)(2,1)} %data.1), custom_call_target="tpu_custom_call" | custom-call | tf_op jit(solution)/shard_map/pallas_call | solution.py:258
  69.6 2.1 %copy.6 = bf16[6,256,256]{2,1,0:T(8,128)(2,1)} copy(bf16[6,256,256]{2,1,0:T(8,128)(2,1)} %shard_map.46) | data formatting | bytes 1572864

commit v5 on v4

--- a/solution.py
+++ b/solution.py
@@ -117,7 +117,7 @@
         gathered(PLANE - 1, pa_recv.at[c])
         for h in range(NZ):
             sb[c, h] = ra[c][split(owner[h])[0]]
-        for dz in range(1, NZ):
+        for dz in (2, 1, 3):
             device, _, z, _ = at(0, dz, 0)
             pltpu.make_async_remote_copy(
                 src_ref=sb.at[c, z], dst_ref=rb[c].at[my_z],
@@ -132,7 +132,7 @@
         gathered(NZ - 1, pb_recv.at[c])
         mine = unit(my_y, c) + my_z
         win[mine] = rb[c][split(owner[my_z])[1]]
-        for dz in range(1, NZ):
+        for dz in (2, 1, 3):
             device = at(0, dz, 0)[0]
             pltpu.make_async_remote_copy(
                 src_ref=win.at[mine], dst_ref=win.at[mine],

time: 72.3 us -> 71.2 us (0.985)
    pallas_call x1, Pallas kernels: 69.5 us -> 68.8 us  [shards(): pl.pallas_call(kernel, out_shape=jax.ShapeDtypeStruct(data.shape, jnp.bfl...]
where the time goes in v5:
time: 71.2 us; the launch traced here: 70.8 us
  Pallas kernels  68.8 us (97%)
  local copies, waits for them, and re-layouts  2.06 us (3%)
    pallas_call x1, Pallas kernels, shards(): pl.pallas_call(kernel, out_shape=jax.ShapeDtypeStruct(data.shape, jnp.bfl...  68.8 us
    unnamed x1, local copies, waits for them, and re-layouts  2.06 us

profile of v5, /device:TPU:2, one launch (start us, length us, event | category | flops | bytes accessed | tf_op | source)
XLA Modules:
  0.0 70.8 jit_solution(11993306372021360306)
XLA Ops:
  0.0 68.8 %shard_map.46 = bf16[6,256,256]{2,1,0:T(8,128)(2,1)} custom-call(s32[4]{0:T(128)} %owner.1, bf16[16,256,256]{2,1,0:T(8,128)(2,1)} %traces.1, bf16[6,16,64]{2,1,0:T(8,128)(2,1)} %prim_in.1, bf16[6,256,256]{2,1,0:T(8,128)(2,1)} %data.1), custom_call_target="tpu_custom_call" | custom-call | tf_op jit(solution)/shard_map/pallas_call | solution.py:258
  68.8 2.1 %copy.6 = bf16[6,256,256]{2,1,0:T(8,128)(2,1)} copy(bf16[6,256,256]{2,1,0:T(8,128)(2,1)} %shard_map.46) | data formatting | bytes 1572864
